TPU v7x, 32 devices: a whole 2x2x4 slice. The times are simulated.
32 devices in a mesh: sec: 2 (over y), dev: 16 (over z, x, core).
Axes of the slice: x: 2, y: 2, z: 4, core: 2. Of those that a mesh axis runs over, the one named last changes fastest.
Arguments:
- flow_state: float32 [5, 8, 1024, 512], P(None, None, ('sec', 'dev')), may hold values from -6 to 6
- diffusion: float32 [8, 1024, 512], P(None, ('sec', 'dev')), may hold values from 0.02 to 0.1
- wall_stress: float32 [2, 1024, 512], P(None, ('sec', 'dev')), may hold values from -3 to 3
- batch_counts: int32 [32, 48], P(('sec', 'dev')), may hold values from 1 to 4, 120 in all within a row
- batch_routes: int32 [1536, 1], P(('sec', 'dev')), may hold values from 0 to 31; in each aligned block of 48 rows (0 to 47, 48 to 95, ...) at most 2 rows name the same one
- wall_index: int32 [1536, 4], P(('sec', 'dev')), may hold values from 0 to 16383, as said below
- input_weight: bfloat16 [12, 2048], replicated, may hold values from -1.75 to 1.75
- middle_weight: bfloat16 [2048, 2048], P(('sec', 'dev')), may hold values from -0.125 to 0.125
- output_weight: bfloat16 [2, 2048], replicated, may hold values from -0.125 to 0.125
Outputs:
- new_field: float32 [5, 8, 1024, 512], P(None, None, ('sec', 'dev'))
- new_stress: float32 [2, 1024, 512], P(None, ('sec', 'dev'))
- batch_loss: float32 [32], P(('sec', 'dev'))
- grad_w_in: float32 [12, 2048], replicated
- grad_w_mid: float32 [2048, 2048], P(('sec', 'dev'))
Inputs may be any that keep to these rules, and one draw needn't show every extreme that they name: `batch_routes`: within the 48 rows of one device no trainer is named more than 2 times, and every trainer is named by some row. `batch_counts`: each device's row sums to 120. `wall_index`: all entries of the 48 rows of one device are distinct.
All inputs are finite; a program needn't handle non-finite values.
Results may differ from a plain program's by a relative error of at most 0.00091.
Values may be sent and summed in bfloat16 or wider, within the bound.
No kernel may reach another device: no remote copies, remote signals or barrier semaphores. Data moves between devices by JAX's collectives and lax.ppermute only.
A program may use at most 128 MiB of HBM per device.

v0:
```python
import math
import jax
import jax.numpy as jnp
from jax import lax
from jax.sharding import PartitionSpec as P

SLOTS = 2
advect_number = 0.3
wall_gain = 0.5
grad_number = 32.0


def extended(block, sides, width):
    for axis, dim in sides:
        count = lax.axis_size(axis)
        forward = [(i, i + 1) for i in range(count - 1)]
        forward.append((count - 1, 0))
        backward = [(target, source) for source, target in forward]
        low = lax.ppermute(
            lax.slice_in_dim(block, block.shape[dim] - width, None, axis=dim), axis, forward
        )
        high = lax.ppermute(lax.slice_in_dim(block, 0, width, axis=dim), axis, backward)
        block = jnp.concatenate([low, block, high], axis=dim)
    return block


def advance(flow_state, diffusion, below_z, above_z):
    below_x = jnp.concatenate([flow_state[..., :1], flow_state[..., :-1]], axis=3)
    above_x = jnp.concatenate([flow_state[..., 1:], flow_state[..., -1:]], axis=3)
    below_y = jnp.concatenate([flow_state[:, :1], flow_state[:, :-1]], axis=1)
    above_y = jnp.concatenate([flow_state[:, 1:], flow_state[:, -1:]], axis=1)
    spread = below_x + above_x + below_y + above_y + below_z + above_z - 6.0 * flow_state
    return flow_state + advect_number * (below_x - flow_state) + diffusion[None] * spread


def wall_columns(flow_state):
    points = flow_state.shape[2] * flow_state.shape[3]
    inputs = flow_state[0:4, 0:3].reshape(12, points)
    targets = jnp.stack(
        [flow_state[1, 4] - flow_state[1, 3], flow_state[3, 4] - flow_state[3, 3]]
    ).reshape(2, points)
    return jnp.concatenate([inputs, targets], axis=0).astype(jnp.bfloat16)


def apply_wall(advanced, new_stress):
    advanced = advanced.at[1, 0].add(-wall_gain * new_stress[0])
    return advanced.at[3, 0].add(-wall_gain * new_stress[1])


def contract_first(left, right):
    return lax.dot_general(
        left, right, (((0,), (0,)), ((), ())), preferred_element_type=jnp.float32
    )


def contract_last(left, right):
    return lax.dot_general(
        left, right, (((1,), (1,)), ((), ())), preferred_element_type=jnp.float32
    )


def body(
    flow_state,
    diffusion,
    wall_stress,
    batch_counts,
    batch_routes,
    wall_index,
    input_weight,
    middle_weight,
    output_weight,
):
    tile_count, capacity = wall_index.shape
    devices = lax.axis_size(("sec", "dev"))
    channels = 14
    slot_total = devices * SLOTS
    row_total = slot_total * capacity
    points = flow_state.shape[2] * flow_state.shape[3]
    columns = wall_columns(flow_state)
    picked = jnp.take(columns, wall_index.reshape(-1), axis=1).reshape(
        channels, tile_count, capacity
    )
    is_live = (
        jnp.arange(capacity, dtype=jnp.int32)[None, :] < batch_counts.reshape(tile_count)[:, None]
    )
    picked = jnp.where(is_live[None], picked, jnp.zeros((), jnp.bfloat16))
    destination = batch_routes.reshape(tile_count)
    matches = (destination[:, None] == jnp.arange(devices, dtype=jnp.int32)[None, :]).astype(
        jnp.int32
    )
    slot_rank = jnp.sum((jnp.cumsum(matches, axis=0) - matches) * matches, axis=1)
    slot_id = destination * SLOTS + slot_rank
    placing = (slot_id[:, None] == jnp.arange(slot_total, dtype=jnp.int32)[None, :]).astype(
        jnp.bfloat16
    )
    send_rows = jnp.einsum(
        "bs,cbk->sck", placing, picked, preferred_element_type=jnp.float32
    ).astype(jnp.bfloat16)
    send_rows = send_rows.reshape(devices, SLOTS, channels, capacity)
    send_live = jnp.einsum(
        "bs,bk->sk", placing, is_live.astype(jnp.bfloat16), preferred_element_type=jnp.float32
    ).astype(jnp.bfloat16)
    send_live = send_live.reshape(devices, SLOTS, capacity)
    got_rows, got_live = (
        lax.all_to_all(send_rows, ("sec", "dev"), split_axis=0, concat_axis=0, tiled=True),
        lax.all_to_all(send_live, ("sec", "dev"), split_axis=0, concat_axis=0, tiled=True),
    )
    sample_rows = jnp.transpose(got_rows, (0, 1, 3, 2)).reshape(row_total, channels)
    features = sample_rows[:, :12]
    targets = sample_rows[:, 12:].astype(jnp.float32)
    live_rows = got_live.reshape(row_total).astype(jnp.float32)
    pre_first = jnp.dot(features, input_weight, preferred_element_type=jnp.float32)
    first_tanh = jnp.tanh(pre_first)
    first_act = first_tanh.astype(jnp.bfloat16)
    part = first_act
    pre_second = jnp.dot(
        part,
        lax.all_gather(middle_weight, ("sec", "dev"), axis=0, tiled=True),
        preferred_element_type=jnp.float32,
    )
    second_tanh = jnp.tanh(pre_second)
    second_act = second_tanh.astype(jnp.bfloat16)
    prediction = contract_last(second_act, output_weight)
    errors = (prediction - targets) * live_rows[:, None]
    sent_back = jnp.transpose(
        prediction.astype(jnp.bfloat16).reshape(devices, SLOTS, capacity, 2), (0, 1, 3, 2)
    )
    answers = lax.all_to_all(sent_back, ("sec", "dev"), split_axis=0, concat_axis=0, tiled=True)
    answers = answers.reshape(slot_total, 2, capacity)
    live_total = jnp.sum(live_rows)
    batch_loss = (0.5 * jnp.sum(errors * errors) / live_total).reshape(1)
    live_dev = 5 * tile_count * capacity // 8
    scale = grad_number / math.sqrt(live_dev * devices)
    back_out = (errors * scale).astype(jnp.bfloat16)
    back_second = (
        jnp.dot(back_out, output_weight, preferred_element_type=jnp.float32)
        * (1.0 - second_tanh * second_tanh)
    ).astype(jnp.bfloat16)
    back_hidden = contract_last(
        back_second, lax.all_gather(middle_weight, ("sec", "dev"), axis=0, tiled=True)
    )
    back_first = (back_hidden * (1.0 - first_tanh * first_tanh)).astype(jnp.bfloat16)
    part = first_act
    grad_w_mid = lax.psum_scatter(
        contract_first(part, back_second), ("sec", "dev"), scatter_dimension=0, tiled=True
    )
    grad_w_in = lax.psum(contract_first(features, back_first), ("sec", "dev"))
    per_tile = jnp.einsum("bs,sck->cbk", placing, answers, preferred_element_type=jnp.float32)
    target_index = jnp.where(is_live, wall_index, points).reshape(-1)
    new_stress = (
        wall_stress.reshape(2, points)
        .at[:, target_index]
        .set(per_tile.reshape(2, -1), mode="drop")
        .reshape(wall_stress.shape)
    )
    padded = extended(flow_state.astype(jnp.bfloat16), ((("sec", "dev"), 2),), 1).astype(
        flow_state.dtype
    )
    advanced = advance(flow_state, diffusion, padded[:, :, :-2], padded[:, :, 2:])
    new_field = apply_wall(advanced, new_stress)
    return (new_field, new_stress, batch_loss, grad_w_in, grad_w_mid)


def solution(mesh):
    in_specs = (
        P(None, None, ("sec", "dev"), None),
        P(None, ("sec", "dev"), None),
        P(None, ("sec", "dev"), None),
        P(("sec", "dev"), None),
        P(("sec", "dev"), None),
        P(("sec", "dev"), None),
        P(),
        P(("sec", "dev"), None),
        P(),
    )
    out_specs = (
        P(None, None, ("sec", "dev"), None),
        P(None, ("sec", "dev"), None),
        P(("sec", "dev")),
        P(),
        P(("sec", "dev"), None),
    )
    return jax.shard_map(body, mesh=mesh, in_specs=in_specs, out_specs=out_specs, check_vma=False)
```

profile of v0, /device:TPU:9, one launch (start us, length us, event | category | flops | bytes accessed | tf_op | source)
XLA Modules:
  0.0 425.7 jit_solution(3434637611886213195)
XLA Ops:
  7.2 0.7 all-gather.2.cloned.1.call-update
  7.9 0.8 fusion.25
  8.8 0.8 select_reduce_fusion
  9.6 0.7 fusion.36
  10.3 0.8 convolution_convert_fusion.1
  11.2 0.7 copy.49
  11.9 6.3 %all-to-all-start.2 = ((bf16[32,2,4]{2,1,0:T(2,128)(2,1)}), bf16[32,2,4]{2,1,0:T(2,128)(2,1)S(1)}, u32[]{:S(2)}, u32[]{:S(2)}) async-start(bf16[32,2,4]{2,1,0:T(2,128)(2,1)} %bitcast.18), calls=%async_computation.2 | async-start | bytes 32768 | tf_op jit(solution)/shard_map/all_to_all | solution.py:106
  18.2 0.8 copy.37
  19.1 2.0 convert_element_type.52
  21.3 1.0 copy-done.3
  22.3 0.3 copy.53
  22.6 0.2 pad_maximum_fusion.1
  22.9 3.4 copy.38
  26.3 3.4 gather_fusion
  29.8 0.2 convolution_convert_fusion
  30.0 0.1 copy.40
  30.2 0.7 copy.41
  30.8 5.8 %all-to-all-start = ((bf16[32,2,14,4]{2,1,3,0:T(2,128)(2,1)}), bf16[32,2,14,4]{2,1,3,0:T(2,128)(2,1)S(1)}, u32[]{:S(2)}, u32[]{:S(2)}) async-start(bf16[32,2,14,4]{2,1,3,0:T(2,128)(2,1)} %copy.41), calls=%async_computation | async-start | bytes 131072 | tf_op jit(solution)/shard_map/all_to_all | solution.py:105
  36.9 5.8 %all-to-all-done = bf16[32,2,14,4]{2,1,3,0:T(2,128)(2,1)S(1)} async-done(((bf16[32,2,14,4]{2,1,3,0:T(2,128)(2,1)}), bf16[32,2,14,4]{2,1,3,0:T(2,128)(2,1)S(1)}, u32[]{:S(2)}, u32[]{:S(2)}) %all-to-all-start) | async-done | bytes 7200 | tf_op jit(solution)/shard_map/all_to_all | solution.py:105
  42.9 1.8 convolution_tanh_fusion.1
  44.6 44.9 %all-gather.2.cloned.1.call-done = bf16[2048,2048]{1,0:T(8,128)(2,1)} async-done(((bf16[64,2048]{1,0:T(8,128)(2,1)}), bf16[2048,2048]{1,0:T(8,128)(2,1)}) %all-gather.2.cloned.1.call-update) | async-done | bytes 8388624 | tf_op jit(solution)/shard_map/all_gather | solution.py:118
  89.6 6.4 %convolution_tanh_fusion = f32[256,2048]{1,0:T(8,128)S(1)} fusion(bf16[2048,2048]{1,0:T(8,128)(2,1)} %all-gather.2.cloned.1.call-done, f32[256,2048]{1,0:T(8,128)} %convolution_tanh_fusion.1), kind=kOutput, calls=%fused_computation.8 | convolution fusion | flops 2148007936 | bytes 12582912 | tf_op jit(solution)/shard_map/dot_general | solution.py:116
  96.0 1.0 multiply_reduce_fusion
  97.0 1.5 fusion.8
  98.4 7.4 %fusion.9 = f32[12,2048]{1,0:T(8,128)} fusion(bf16[256,2048]{1,0:T(8,128)(2,1)} %fusion.8, bf16[2048,2048]{1,0:T(8,128)(2,1)} %all-gather.2.cloned.1.call-done, f32[256,2048]{1,0:T(8,128)} %convolution_tanh_fusion.1, bf16[256,14]{1,0:T(8,128)(2,1)S(1)} %bitcast.59), kind=kOutput, calls=%fused_computation.22 | convolution fusion | flops 2162163712 | bytes 11639808 | tf_op jit(solution)/shard_map/dot_general | solution.py:51
  105.9 10.0 %fusion.13 = f32[2048,2048]{1,0:T(8,128)} fusion(bf16[256,2048]{1,0:T(8,128)(2,1)} %fusion.8, f32[256,2048]{1,0:T(8,128)} %convolution_tanh_fusion.1), kind=kOutput, calls=%fused_computation.30 | convolution fusion | flops 2148007936 | bytes 19922944 | tf_op jit(solution)/shard_map/dot_general | solution.py:51
  115.9 1.3 fusion.45
  117.2 1.3 collective-permute-start
  118.7 4.6 %copy.35 = f32[2,32,512]{0,2,1:T(8,128)} copy(f32[2,32,512]{2,1,0:T(8,128)S(1)} %copy-done.5) | data formatting | bytes 262144 | tf_op args[2]
  123.4 0.9 fusion.44
  124.3 1.1 fusion.41
  125.4 2.8 fusion.43
  128.2 3.4 fusion.42
  131.7 0.6 convert_reduce_fusion
  132.3 3.4 maximum_convert_fusion
  135.8 0.6 copy.43
  136.4 6.6 %all-to-all-start.1 = ((bf16[32,2,2,4]{3,1,2,0:T(2,128)(2,1)}), bf16[32,2,2,4]{3,1,2,0:T(2,128)(2,1)S(1)}, u32[]{:S(2)}, u32[]{:S(2)}) async-start(bf16[32,2,2,4]{3,1,2,0:T(2,128)(2,1)} %copy.43), calls=%async_computation.1 | async-start | bytes 65536 | tf_op jit(solution)/shard_map/all_to_all | solution.py:128
  143.1 9.2 %fusion.4 = f32[5,8,32,512]{3,2,1,0:T(8,128)} fusion(f32[5,8,34,512]{3,2,1,0:T(8,128)} %maximum_convert_fusion, f32[5,8,32,1]{3,2,1,0:T(8,128)} %get-tuple-element.49, f32[5,8,32,511]{3,2,1,0:T(8,128)} %get-tuple-element.51, f32[5,7,32,512]{3,2,1,0:T(8,128)} %get-tuple-element.53, f32[5,1,32,512]{3,2,1,0:T(8,128)} %get-tuple-element.55, ...), kind=kLoop, calls=%fused_computation.13 | loop fusion | flops 10485760 | bytes 21495808 | tf_op jit(solution)/shard_map/add | solution.py:33
  153.7 0.2 convolution_bitcast_fusion
  154.1 0.1 copy.47
  154.2 7.6 %scatter_fusion = f32[2,16384]{0,1:T(8,128)} fusion(f32[2,16384]{0,1:T(8,128)} %bitcast.52, s32[192]{0:T(256)S(1)} %bitcast.68, f32[192,2]{1,0:T(8,128)S(1)} %copy.47), kind=kCustom, calls=%fused_computation.1 | custom fusion | bytes 5376 | tf_op jit(solution)/shard_map/scatter | solution.py:153
  161.8 5.9 %copy.50 = f32[2,32,512]{2,1,0:T(8,128)} copy(f32[2,32,512]{0,2,1:T(8,128)} %bitcast.53) | data formatting | bytes 262144
  167.7 12.3 %fusion = (f32[16384]{0:T(1024)S(1)}, f32[16384]{0:T(1024)S(1)}) fusion(f32[2,16384]{0,1:T(8,128)} %scatter_fusion), kind=kLoop, calls=%fused_computation.3 | loop fusion | flops 32768 | bytes 262144 | tf_op jit(solution)/shard_map/mul | solution.py:47
  180.0 1.5 fusion.17
  181.5 1.5 fusion.16
  183.0 43.7 %all-reduce.2.cloned.1.call-done = f32[12,2048]{1,0:T(8,128)} async-done(((f32[12,2048]{1,0:T(8,128)}), f32[12,2048]{1,0:T(8,128)}) %all-reduce.2.cloned.1.call-update) | async-done | bytes 98320 | tf_op jit(solution)/shard_map/psum | solution.py:147
  226.7 189.8 %reduce-scatter.2.cloned.1.call-done = f32[64,2048]{1,0:T(8,128)} async-done(((f32[2048,2048]{1,0:T(8,128)}), f32[64,2048]{1,0:T(8,128)}) %reduce-scatter.2.cloned.1.call-update) | async-done | bytes 524304 | tf_op jit(solution)/shard_map/reduce_scatter | solution.py:144
  416.5 1.6 copy.60
  (52 shorter events, 1.6 us)
Async XLA Ops:
  7.2 35.7 %copy-start = (bf16[12,2048]{1,0:T(8,128)(2,1)S(1)}, bf16[12,2048]{1,0:T(8,128)(2,1)}, u32[]{:S(2)}) copy-start(bf16[12,2048]{1,0:T(8,128)(2,1)} %param.19) | copy-start | bytes 147460
  7.2 13.9 %copy-start.2 = (f32[5,8,32,512]{3,2,1,0:T(8,128)S(1)}, f32[5,8,32,512]{3,2,1,0:T(8,128)}, u32[]{:S(2)}) copy-start(f32[5,8,32,512]{3,2,1,0:T(8,128)} %param.13) | copy-start | bytes 7864324
  7.2 82.4 %all-gather.2.cloned.1.call-start = ((), (), s32[]{:S(2)}) async-start(), calls=%async_computation.4 | async-start | bytes 8650752 | tf_op jit(solution)/shard_map/all_gather | solution.py:118
  11.9 19.0 %all-to-all-start.2 = ((bf16[32,2,4]{2,1,0:T(2,128)(2,1)}), bf16[32,2,4]{2,1,0:T(2,128)(2,1)S(1)}, u32[]{:S(2)}, u32[]{:S(2)}) async-start(bf16[32,2,4]{2,1,0:T(2,128)(2,1)} %bitcast.18), calls=%async_computation.2 | async-start | bytes 32768 | tf_op jit(solution)/shard_map/all_to_all | solution.py:106
  21.1 1.2 copy-start.3
  22.9 6.9 %copy-start.7 = (s32[48,4]{0,1:T(4,128)S(1)}, s32[48,4]{0,1:T(4,128)}, u32[]{:S(2)}) copy-start(s32[48,4]{0,1:T(4,128)} %param.18) | copy-start | bytes 2308
  22.9 6.9 %copy-start.8 = (s32[1,48]{1,0:T(1,128)S(1)}, s32[1,48]{1,0:T(1,128)}, u32[]{:S(2)}) copy-start(s32[1,48]{1,0:T(1,128)} %param.16) | copy-start | bytes 580
  30.8 11.8 %all-to-all-start = ((bf16[32,2,14,4]{2,1,3,0:T(2,128)(2,1)}), bf16[32,2,14,4]{2,1,3,0:T(2,128)(2,1)S(1)}, u32[]{:S(2)}, u32[]{:S(2)}) async-start(bf16[32,2,14,4]{2,1,3,0:T(2,128)(2,1)} %copy.41), calls=%async_computation | async-start | bytes 131072 | tf_op jit(solution)/shard_map/all_to_all | solution.py:105
  36.7 190.0 %all-reduce.2.cloned.1.call-start = ((), (), s32[]{:S(2)}) async-start(), calls=%async_computation.5 | async-start | bytes 262144 | tf_op jit(solution)/shard_map/psum | solution.py:147
  44.6 51.3 %copy-start.6 = (bf16[2,2048]{1,0:T(2,128)(2,1)S(1)}, bf16[2,2048]{1,0:T(2,128)(2,1)}, u32[]{:S(2)}) copy-start(bf16[2,2048]{1,0:T(2,128)(2,1)} %param.21) | copy-start | bytes 24580
  105.9 310.7 %reduce-scatter.2.cloned.1.call-start = ((), (), s32[]{:S(2)}) async-start(), calls=%async_computation.6 | async-start | bytes 17301504 | tf_op jit(solution)/shard_map/reduce_scatter | solution.py:144
  115.9 2.8 copy-start.5
  117.2 15.1 %collective-permute-start = (bf16[5,8,1,512]{3,2,1,0:T(2,128)(2,1)S(1)}, bf16[5,8,1,512]{3,2,1,0:T(2,128)(2,1)}, u32[]{:S(2)}, u32[]{:S(2)}) collective-permute-start(bf16[5,8,1,512]{3,2,1,0:T(2,128)(2,1)S(1)} %get-tuple-element.56), channel_id=1, source_target_pairs={{0,1},{1,2},{2,3},{3,4},{4,5},{5,6},{6,7},{7,8},{8,9},{9,10},{10,1... | collective-permute-start | bytes 122888 | tf_op jit(solution)/shard_map/ppermute | solution.py:19
  118.5 13.8 %collective-permute-start.1 = (bf16[5,8,1,512]{3,2,1,0:T(2,128)(2,1)S(1)}, bf16[5,8,1,512]{3,2,1,0:T(2,128)(2,1)}, u32[]{:S(2)}, u32[]{:S(2)}) collective-permute-start(bf16[5,8,1,512]{3,2,1,0:T(2,128)(2,1)S(1)} %get-tuple-element.57), channel_id=1, source_target_pairs={{1,0},{2,1},{3,2},{4,3},{5,4},{6,5},{7,6},{8,7},{9,8},{10,9},{11,1... | collective-permute-start | bytes 122888 | tf_op jit(solution)/shard_map/ppermute | solution.py:22
  128.2 4.1 copy-start.4
  136.4 17.2 %all-to-all-start.1 = ((bf16[32,2,2,4]{3,1,2,0:T(2,128)(2,1)}), bf16[32,2,2,4]{3,1,2,0:T(2,128)(2,1)S(1)}, u32[]{:S(2)}, u32[]{:S(2)}) async-start(bf16[32,2,2,4]{3,1,2,0:T(2,128)(2,1)} %copy.43), calls=%async_computation.1 | async-start | bytes 65536 | tf_op jit(solution)/shard_map/all_to_all | solution.py:128
  167.7 250.4 %copy-start.1 = (bf16[12,2048]{1,0:T(8,128)(2,1)S(1)}, bf16[12,2048]{1,0:T(8,128)(2,1)}, u32[]{:S(2)}) copy-start(bf16[12,2048]{1,0:T(8,128)(2,1)} %param.19) | copy-start | bytes 147460
Sparse Core Ops, SparseCore 0:
  10.8 78.7 all-gather.1
  106.0 120.6 all-reduce.1
  229.6 186.8 reduce-scatter.1
where the time goes:
time: 426 us
  waiting for transfers between devices  285 us (67%)
  local copies, waits for them, and re-layouts  41.6 us (10%)
  other arithmetic  33.1 us (8%)
  matrix products  29.2 us (7%)
  starting transfers between devices  20.3 us (5%)
  between operations  16.5 us (4%)
    reduce_scatter x1, waiting for transfers between devices, body(): lax.psum_scatter(contract_first(part, back_second), ('sec', 'dev'), scatt...  190 us
    all_gather x1, waiting for transfers between devices, body(): lax.all_gather(middle_weight, ('sec', 'dev'), axis=0, tiled=True)  44.9 us
    psum x1, waiting for transfers between devices, body(): grad_w_in = lax.psum(contract_first(features, back_first), ('sec', 'dev'))  43.7 us
    dot_general x2, matrix products, contract_first(): lax.dot_general(left, right, (((0,), (0,)), ((), ())), preferred_element_...  17.4 us
    unnamed x27, local copies, waits for them, and re-layouts  14.4 us
    mul x1, other arithmetic, apply_wall(): return advanced.at[3, 0].add(-wall_gain * new_stress[1])  12.3 us
    add x1, other arithmetic, advance(): flow_state + advect_number * (below_x - flow_state)  9.22 us
  transfers between devices with their start and end apart: 8, of which 4 were waited for; matrix products, arithmetic and copies ran while one was open for 20% of the time, Pallas kernels for 0%

commit v1 on v0

--- a/solution.py
+++ b/solution.py
@@ -8,6 +8,23 @@
 advect_number = 0.3
 wall_gain = 0.5
 grad_number = 32.0
+
+
+def form_turns(matrix):
+    mesh_ax = ("sec", "dev")
+    local_out = jax.lax.psum(1, mesh_ax)
+    now = jax.lax.axis_index(mesh_ax)
+    carry_out, view_out, y = (local_out, now, matrix.shape[0])
+    front, fresh = (matrix, 1)
+    while fresh < carry_out:
+        queue = []
+        for at in range(carry_out):
+            queue.append((at, (at - fresh) % carry_out))
+        parts_out = jax.lax.ppermute(front, mesh_ax, queue)
+        front = jnp.concatenate([front, parts_out], axis=0)
+        fresh = 2 * fresh
+    val2 = jnp.roll(front, view_out * y, axis=0)
+    return val2
 
 
 def extended(block, sides, width):
@@ -113,11 +130,7 @@
     first_tanh = jnp.tanh(pre_first)
     first_act = first_tanh.astype(jnp.bfloat16)
     part = first_act
-    pre_second = jnp.dot(
-        part,
-        lax.all_gather(middle_weight, ("sec", "dev"), axis=0, tiled=True),
-        preferred_element_type=jnp.float32,
-    )
+    pre_second = jnp.dot(part, form_turns(middle_weight), preferred_element_type=jnp.float32)
     second_tanh = jnp.tanh(pre_second)
     second_act = second_tanh.astype(jnp.bfloat16)
     prediction = contract_last(second_act, output_weight)

time: 426 us -> 653 us (1.53)
  waiting for transfers between devices: 285 us -> 461 us
  local copies, waits for them, and re-layouts: 41.6 us -> 70.4 us
  starting transfers between devices: 20.3 us -> 42.5 us
    ppermute x0 -> x5, waiting for transfers between devices: none -> 159 us  [form_turns(): parts_out = jax.lax.ppermute(front, mesh_ax, queue)]
    all_to_all x1, waiting for transfers between devices: 0.01 us -> 64.7 us  [body(): lax.all_to_all(send_live, ('sec', 'dev'), split_axis=0, concat_axis=0, ti...]
    all_gather x1, waiting for transfers between devices: 44.9 us -> 0.01 us  [body(): lax.all_gather(middle_weight, ('sec', 'dev'), axis=0, tiled=True)]
    unnamed x27 -> x69, local copies, waits for them, and re-layouts: 14.4 us -> 31.3 us
    ppermute x0 -> x5, starting transfers between devices: none -> 12 us  [form_turns(): parts_out = jax.lax.ppermute(front, mesh_ax, queue)]
    concatenate x0 -> x2, local copies, waits for them, and re-layouts: none -> 7.28 us  [the longest x1 4.7 us: form_turns(): val2 = jnp.roll(front, view_out * y, axis=0)]
  transfers between devices with their start and end apart: 8 -> 13, of which waited for: 4 -> 8; matrix products, arithmetic and copies ran while one was open for 20% -> 19% of each run, Pallas kernels for 0% -> 0%
where the time goes in v1:
time: 653 us; the launch traced here: 652 us
  waiting for transfers between devices  461 us (71%)
  local copies, waits for them, and re-layouts  70.4 us (11%)
  starting transfers between devices  42.5 us (7%)
  other arithmetic  33.6 us (5%)
  matrix products  28 us (4%)
  between operations  16.6 us (3%)
    reduce_scatter x1, waiting for transfers between devices, body(): lax.psum_scatter(contract_first(part, back_second), ('sec', 'dev'), scatt...  190 us
    ppermute x5, waiting for transfers between devices, form_turns(): parts_out = jax.lax.ppermute(front, mesh_ax, queue)  159 us
    all_to_all x1, waiting for transfers between devices, body(): lax.all_to_all(send_live, ('sec', 'dev'), split_axis=0, concat_axis=0, ti...  64.7 us
    psum x1, waiting for transfers between devices, body(): grad_w_in = lax.psum(contract_first(features, back_first), ('sec', 'dev'))  41.7 us
    unnamed x69, local copies, waits for them, and re-layouts  31.3 us
    dot_general x2, matrix products, contract_first(): lax.dot_general(left, right, (((0,), (0,)), ((), ())), preferred_element_...  17.4 us
  transfers between devices with their start and end apart: 13, of which 8 were waited for; matrix products, arithmetic and copies ran while one was open for 19% of the time, Pallas kernels for 0%

profile of v1, /device:TPU:9, one launch (start us, length us, event | category | flops | bytes accessed | tf_op | source)
XLA Modules:
  0.0 651.9 jit_solution(13470376155071554720)
XLA Ops:
  8.7 5.4 collective-permute-done.2
  14.0 1.1 pad_maximum_fusion.4
  15.1 2.0 collective-permute-start.3
  17.1 14.7 %collective-permute-done.3 = bf16[128,2048]{1,0:T(8,128)(2,1)S(1)} collective-permute-done((bf16[128,2048]{1,0:T(8,128)(2,1)S(1)}, bf16[128,2048]{1,0:T(8,128)(2,1)S(1)}, u32[]{:S(2)}, u32[]{:S(2)}) %collective-permute-start.3) | collective-permute-done | bytes 524320 | tf_op jit(solution)/shard_map/ppermute | solution.py:23
  31.9 1.0 pad_maximum_fusion.2
  32.9 5.6 collective-permute-start.4
  38.5 21.2 %collective-permute-done.4 = bf16[256,2048]{1,0:T(8,128)(2,1)S(1)} collective-permute-done((bf16[256,2048]{1,0:T(8,128)(2,1)S(1)}, bf16[256,2048]{1,0:T(8,128)(2,1)S(1)}, u32[]{:S(2)}, u32[]{:S(2)}) %collective-permute-start.4) | collective-permute-done | bytes 1048608 | tf_op jit(solution)/shard_map/ppermute | solution.py:23
  59.9 3.4 collective-permute-start.5
  65.1 1.1 constant_dynamic-update-slice_fusion.2
  66.2 1.6 constant_dynamic-update-slice_fusion.1
  67.8 117.3 %collective-permute-done.5 = bf16[512,2048]{1,0:T(8,128)(2,1)S(1)} collective-permute-done((bf16[512,2048]{1,0:T(8,128)(2,1)S(1)}, bf16[512,2048]{1,0:T(8,128)(2,1)S(1)}, u32[]{:S(2)}, u32[]{:S(2)}) %collective-permute-start.5) | collective-permute-done | bytes 2097184 | tf_op jit(solution)/shard_map/ppermute | solution.py:23
  185.1 2.6 constant_dynamic-update-slice_fusion
  189.6 10.6 %all-to-all-start.2 = ((bf16[32,2,4]{2,1,0:T(2,128)(2,1)}), bf16[32,2,4]{2,1,0:T(2,128)(2,1)S(1)}, u32[]{:S(2)}, u32[]{:S(2)}) async-start(bf16[32,2,4]{2,1,0:T(2,128)(2,1)} %bitcast.18), calls=%async_computation.2 | async-start | bytes 32768 | tf_op jit(solution)/shard_map/all_to_all | solution.py:123
  200.5 1.0 copy-done.9
  202.1 1.0 pad_maximum_fusion.3
  203.1 4.6 copy.38
  208.7 3.4 gather_fusion
  213.5 1.5 convolution_convert_fusion
  216.6 64.7 %all-to-all-done.2 = bf16[32,2,4]{2,1,0:T(2,128)(2,1)S(1)} async-done(((bf16[32,2,4]{2,1,0:T(2,128)(2,1)}), bf16[32,2,4]{2,1,0:T(2,128)(2,1)S(1)}, u32[]{:S(2)}, u32[]{:S(2)}) %all-to-all-start.2) | async-done | bytes 544 | tf_op jit(solution)/shard_map/all_to_all | solution.py:123
  281.2 10.3 %all-to-all-start = ((bf16[32,2,14,4]{2,1,3,0:T(2,128)(2,1)}), bf16[32,2,14,4]{2,1,3,0:T(2,128)(2,1)S(1)}, u32[]{:S(2)}, u32[]{:S(2)}) async-start(bf16[32,2,14,4]{2,1,3,0:T(2,128)(2,1)} %copy.41), calls=%async_computation | async-start | bytes 131072 | tf_op jit(solution)/shard_map/all_to_all | solution.py:122
  292.3 5.2 all-to-all-done
  299.7 1.5 copy.52
  301.6 5.6 constant_dynamic-update-slice_fusion.11
  309.5 1.1 constant_dynamic-update-slice_fusion.7
  310.6 1.5 constant_dynamic-update-slice_fusion.6
  312.1 4.7 constant_dynamic-update-slice_fusion.5
  316.8 5.8 fusion.4
  322.6 1.0 multiply_reduce_fusion
  323.6 1.5 multiply_convert_fusion
  325.1 7.4 %fusion.13 = f32[12,2048]{1,0:T(8,128)} fusion(bf16[256,2048]{1,0:T(8,128)(2,1)} %multiply_convert_fusion, bf16[2048,2048]{1,0:T(8,128)(2,1)} %all-gather.2.cloned.1.call-done, f32[256,2048]{1,0:T(8,128)} %copy-done.8, bf16[256,14]{1,0:T(8,128)(2,1)S(1)} %bitcast.57), kind=kOutput, calls=%fused_computation.24 | convolution fusion | flops 2162163712 | bytes 11639808 | tf_op jit(solution)/shard_map/dot_general | solution.py:68
  332.8 10.0 %fusion.17 = f32[2048,2048]{1,0:T(8,128)} fusion(bf16[256,2048]{1,0:T(8,128)(2,1)} %multiply_convert_fusion, f32[256,2048]{1,0:T(8,128)} %copy-done.8), kind=kOutput, calls=%fused_computation.34 | convolution fusion | flops 2148007936 | bytes 19922944 | tf_op jit(solution)/shard_map/dot_general | solution.py:68
  342.8 1.3 fusion.51
  344.1 1.0 collective-permute-start
  345.1 4.7 copy.35
  350.7 1.1 fusion.47
  351.8 2.8 fusion.49
  354.6 3.4 fusion.48
  358.7 3.3 maximum_convert_fusion
  362.7 8.3 %all-to-all-start.1 = ((bf16[32,2,2,4]{3,1,2,0:T(2,128)(2,1)}), bf16[32,2,2,4]{3,1,2,0:T(2,128)(2,1)S(1)}, u32[]{:S(2)}, u32[]{:S(2)}) async-start(bf16[32,2,2,4]{3,1,2,0:T(2,128)(2,1)} %copy.43), calls=%async_computation.1 | async-start | bytes 65536 | tf_op jit(solution)/shard_map/all_to_all | solution.py:141
  371.0 9.2 %fusion.9 = f32[5,8,32,512]{3,2,1,0:T(8,128)} fusion(f32[5,8,34,512]{3,2,1,0:T(8,128)} %maximum_convert_fusion, f32[5,8,32,1]{3,2,1,0:T(8,128)} %get-tuple-element.49, f32[5,8,32,511]{3,2,1,0:T(8,128)} %get-tuple-element.51, f32[5,7,32,512]{3,2,1,0:T(8,128)} %get-tuple-element.53, f32[5,1,32,512]{3,2,1,0:T(8,128)} %get-tuple-element.55, ...), kind=kLoop, calls=%fused_computation.14 | loop fusion | flops 10485760 | bytes 21495808 | tf_op jit(solution)/shard_map/add | solution.py:50
  382.2 7.7 %scatter_fusion = f32[2,16384]{0,1:T(8,128)} fusion(f32[2,16384]{0,1:T(8,128)} %bitcast.50, s32[192]{0:T(256)S(1)} %bitcast.66, f32[192,2]{1,0:T(8,128)S(1)} %copy.47), kind=kCustom, calls=%fused_computation.1 | custom fusion | bytes 5376 | tf_op jit(solution)/shard_map/scatter | solution.py:166
  389.8 12.4 %fusion = (f32[16384]{0:T(1024)S(1)}, f32[16384]{0:T(1024)S(1)}) fusion(f32[2,16384]{0,1:T(8,128)} %scatter_fusion), kind=kLoop, calls=%fused_computation.3 | loop fusion | flops 32768 | bytes 262144 | tf_op jit(solution)/shard_map/mul | solution.py:64
  402.3 5.9 copy.50
  408.2 1.5 fusion.21
  409.7 1.5 fusion.20
  411.2 41.7 %all-reduce.2.cloned.1.call-done = f32[12,2048]{1,0:T(8,128)} async-done(((f32[12,2048]{1,0:T(8,128)}), f32[12,2048]{1,0:T(8,128)}) %all-reduce.2.cloned.1.call-update) | async-done | bytes 98320 | tf_op jit(solution)/shard_map/psum | solution.py:160
  452.8 189.8 %reduce-scatter.2.cloned.1.call-done = f32[64,2048]{1,0:T(8,128)} async-done(((f32[2048,2048]{1,0:T(8,128)}), f32[64,2048]{1,0:T(8,128)}) %reduce-scatter.2.cloned.1.call-update) | async-done | bytes 524304 | tf_op jit(solution)/shard_map/reduce_scatter | solution.py:157
  642.6 1.6 copy.75
  (108 shorter events, 18.7 us)
Async XLA Ops:
  7.2 294.0 %copy-start = (bf16[12,2048]{1,0:T(8,128)(2,1)S(1)}, bf16[12,2048]{1,0:T(8,128)(2,1)}, u32[]{:S(2)}) copy-start(bf16[12,2048]{1,0:T(8,128)(2,1)} %param.19) | copy-start | bytes 147460
  7.2 52.5 %copy-start.5 = (bf16[64,2048]{1,0:T(8,128)(2,1)S(1)}, bf16[64,2048]{1,0:T(8,128)(2,1)}, u32[]{:S(2)}) copy-start(bf16[64,2048]{1,0:T(8,128)(2,1)} %param.20) | copy-start | bytes 786436
  7.2 317.9 %all-gather.2.cloned.1.call-start = ((), (), s32[]{:S(2)}) async-start(), calls=%async_computation.4 | async-start | bytes 8650752 | tf_op jit(solution)/shard_map/all_gather | solution.py:153
  7.9 6.1 collective-permute-start.2
  14.0 50.2 %copy-start.11 = (bf16[64,2048]{1,0:T(8,128)(2,1)}, bf16[64,2048]{1,0:T(8,128)(2,1)S(1)}, u32[]{:S(2)}) copy-start(bf16[64,2048]{1,0:T(8,128)(2,1)S(1)} %collective-permute-done.2) | copy-start | bytes 786436
  15.1 16.8 %collective-permute-start.3 = (bf16[128,2048]{1,0:T(8,128)(2,1)S(1)}, bf16[128,2048]{1,0:T(8,128)(2,1)S(1)}, u32[]{:S(2)}, u32[]{:S(2)}) collective-permute-start(bf16[128,2048]{1,0:T(8,128)(2,1)S(1)} %pad_maximum_fusion.4), channel_id=1, source_target_pairs={{0,30},{1,31},{2,0},{3,1},{4,2},{5,3},{6,4},{7,5},{8,6},{9,7},{10,... | collective-permute-start | bytes 1572872 | tf_op jit(solution)/shard_map/ppermute | solution.py:23
  32.9 26.8 %collective-permute-start.4 = (bf16[256,2048]{1,0:T(8,128)(2,1)S(1)}, bf16[256,2048]{1,0:T(8,128)(2,1)S(1)}, u32[]{:S(2)}, u32[]{:S(2)}) collective-permute-start(bf16[256,2048]{1,0:T(8,128)(2,1)S(1)} %pad_maximum_fusion.2), channel_id=1, source_target_pairs={{0,28},{1,29},{2,30},{3,31},{4,0},{5,1},{6,2},{7,3},{8,4},{9,5},{1... | collective-permute-start | bytes 3145736 | tf_op jit(solution)/shard_map/ppermute | solution.py:23
  59.7 6.5 copy-start.3
  59.9 125.3 %collective-permute-start.5 = (bf16[512,2048]{1,0:T(8,128)(2,1)S(1)}, bf16[512,2048]{1,0:T(8,128)(2,1)S(1)}, u32[]{:S(2)}, u32[]{:S(2)}) collective-permute-start(bf16[512,2048]{1,0:T(8,128)(2,1)S(1)} %pad_maximum_fusion.1), channel_id=1, source_target_pairs={{0,24},{1,25},{2,26},{3,27},{4,28},{5,29},{6,30},{7,31},{8,0},{9,1... | collective-permute-start | bytes 6291464 | tf_op jit(solution)/shard_map/ppermute | solution.py:23
  185.1 3.0 copy-start.6
  185.1 3.2 copy-start.20
  185.1 3.6 copy-start.21
  185.1 15.1 %copy-start.2 = (f32[5,8,32,512]{3,2,1,0:T(8,128)S(1)}, f32[5,8,32,512]{3,2,1,0:T(8,128)}, u32[]{:S(2)}) copy-start(f32[5,8,32,512]{3,2,1,0:T(8,128)} %param.13) | copy-start | bytes 7864324
  188.1 113.5 %collective-permute-start.6 = (bf16[1024,2048]{1,0:T(8,128)(2,1)}, bf16[1024,2048]{1,0:T(8,128)(2,1)}, u32[]{:S(2)}, u32[]{:S(2)}) collective-permute-start(bf16[1024,2048]{1,0:T(8,128)(2,1)} %get-tuple-element.56), channel_id=1, source_target_pairs={{0,16},{1,17},{2,18},{3,19},{4,20},{5,21},{6,22},{7,23},{8,24},{9,... | collective-permute-start | bytes 12582920 | tf_op jit(solution)/shard_map/ppermute | solution.py:23
  188.7 12.9 %copy-start.23 = (s32[48]{0:T(128)}, s32[48]{0:T(128)S(1)}, u32[]{:S(2)}) copy-start(s32[48]{0:T(128)S(1)} %fusion.42) | copy-start | bytes 580
  189.6 91.6 %all-to-all-start.2 = ((bf16[32,2,4]{2,1,0:T(2,128)(2,1)}), bf16[32,2,4]{2,1,0:T(2,128)(2,1)S(1)}, u32[]{:S(2)}, u32[]{:S(2)}) async-start(bf16[32,2,4]{2,1,0:T(2,128)(2,1)} %bitcast.18), calls=%async_computation.2 | async-start | bytes 32768 | tf_op jit(solution)/shard_map/all_to_all | solution.py:123
  200.5 1.1 copy-start.9
  203.1 4.6 copy-start.16
  203.1 4.7 copy-start.22
  281.2 16.3 %all-to-all-start = ((bf16[32,2,14,4]{2,1,3,0:T(2,128)(2,1)}), bf16[32,2,14,4]{2,1,3,0:T(2,128)(2,1)S(1)}, u32[]{:S(2)}, u32[]{:S(2)}) async-start(bf16[32,2,14,4]{2,1,3,0:T(2,128)(2,1)} %copy.41), calls=%async_computation | async-start | bytes 131072 | tf_op jit(solution)/shard_map/all_to_all | solution.py:122
  291.5 161.3 %all-reduce.2.cloned.1.call-start = ((), (), s32[]{:S(2)}) async-start(), calls=%async_computation.5 | async-start | bytes 262144 | tf_op jit(solution)/shard_map/psum | solution.py:160
  297.5 0.6 copy-start.13
  301.6 15.2 %copy-start.8 = (f32[256,2048]{1,0:T(8,128)}, f32[256,2048]{1,0:T(8,128)S(1)}, u32[]{:S(2)}) copy-start(f32[256,2048]{1,0:T(8,128)S(1)} %convolution_tanh_fusion) | copy-start | bytes 6291460
  301.6 6.3 copy-start.12
  307.2 2.3 copy-start.4
  307.2 3.4 copy-start.7
  316.8 5.8 copy-start.15
  316.8 5.8 copy-start.17
  316.8 5.8 copy-start.18
  332.5 310.1 %reduce-scatter.2.cloned.1.call-start = ((), (), s32[]{:S(2)}) async-start(), calls=%async_computation.6 | async-start | bytes 17301504 | tf_op jit(solution)/shard_map/reduce_scatter | solution.py:157
  342.8 2.3 copy-start.14
  344.1 14.6 %collective-permute-start = (bf16[5,8,1,512]{3,2,1,0:T(2,128)(2,1)S(1)}, bf16[5,8,1,512]{3,2,1,0:T(2,128)(2,1)}, u32[]{:S(2)}, u32[]{:S(2)}) collective-permute-start(bf16[5,8,1,512]{3,2,1,0:T(2,128)(2,1)S(1)} %get-tuple-element.58), channel_id=1, source_target_pairs={{0,1},{1,2},{2,3},{3,4},{4,5},{5,6},{6,7},{7,8},{8,9},{9,10},{10,1... | collective-permute-start | bytes 122888 | tf_op jit(solution)/shard_map/ppermute | solution.py:36
  345.1 13.6 %collective-permute-start.1 = (bf16[5,8,1,512]{3,2,1,0:T(2,128)(2,1)S(1)}, bf16[5,8,1,512]{3,2,1,0:T(2,128)(2,1)}, u32[]{:S(2)}, u32[]{:S(2)}) collective-permute-start(bf16[5,8,1,512]{3,2,1,0:T(2,128)(2,1)S(1)} %get-tuple-element.59), channel_id=1, source_target_pairs={{1,0},{2,1},{3,2},{4,3},{5,4},{6,5},{7,6},{8,7},{9,8},{10,9},{11,1... | collective-permute-start | bytes 122888 | tf_op jit(solution)/shard_map/ppermute | solution.py:39
  354.6 4.0 copy-start.10
  362.7 18.8 %all-to-all-start.1 = ((bf16[32,2,2,4]{3,1,2,0:T(2,128)(2,1)}), bf16[32,2,2,4]{3,1,2,0:T(2,128)(2,1)S(1)}, u32[]{:S(2)}, u32[]{:S(2)}) async-start(bf16[32,2,2,4]{3,1,2,0:T(2,128)(2,1)} %copy.43), calls=%async_computation.1 | async-start | bytes 65536 | tf_op jit(solution)/shard_map/all_to_all | solution.py:141
  371.0 10.6 %copy-start.24 = (s32[48]{0:T(128)S(1)}, s32[48]{0:T(128)}, u32[]{:S(2)}) copy-start(s32[48]{0:T(128)} %copy-done.23) | copy-start | bytes 580
  371.0 11.1 %copy-start.19 = (s32[192,1]{0,1:T(1,128)S(1)}, s32[192,1]{0,1:T(1,128)}, u32[]{:S(2)}) copy-start(s32[192,1]{0,1:T(1,128)} %get-tuple-element.72) | copy-start | bytes 2308
  402.3 241.9 %copy-start.1 = (bf16[12,2048]{1,0:T(8,128)(2,1)S(1)}, bf16[12,2048]{1,0:T(8,128)(2,1)}, u32[]{:S(2)}) copy-start(bf16[12,2048]{1,0:T(8,128)(2,1)} %param.19) | copy-start | bytes 147460
Sparse Core Ops, SparseCore 0:
  10.8 159.3 all-gather.1
  332.7 120.1 all-reduce.1
  455.7 186.8 reduce-scatter.1
